TPU v7x, 128 devices: a whole 4x4x4 slice. The times are simulated.
128 devices in a mesh: ia: 8 (over z, y_hi), ja: 8 (over x, core), aux: 2 (over y_lo).
Axes of the slice: x: 4, y: 4 (y_hi: 2, y_lo: 2; y = y_hi * 2 + y_lo), z: 4, core: 2. Of those that a mesh axis runs over, the one named last changes fastest.
Arguments:
- raw_integrals: bfloat16 [2048, 24, 512], P(('ia', 'ja', 'aux')), may hold values from -0.5 to 0.5
- metric_root: bfloat16 [2048, 2048], replicated, may hold values from -0.125 to 0.125
- eps_occ: float32 [24], replicated, may hold values from -2 to -0.3
- eps_vir: float32 [512], replicated, may hold values from 0.3 to 3
Outputs:
- gamma: float32 [2048, 24, 512], P('ja', 'ia', 'aux')
All inputs are finite; a program needn't handle non-finite values.
Results may differ from a plain program's by a relative error of at most 0.0022.
Values may be sent and summed in bfloat16 or wider, within the bound.
A program may use at most 128 MiB of HBM per device.

v0:
```python
import jax
import jax.numpy as jnp
from jax import lax
from jax.sharding import PartitionSpec as P

OB = 3
V = 512


def sent_together(arrays, axis, split_dim, concat_dim, along):
    widths = [a.shape[along] for a in arrays]
    both = jnp.concatenate(arrays, axis=along)
    result = lax.all_to_all(both, axis, split_axis=split_dim, concat_axis=concat_dim, tiled=True)
    return tuple(jnp.split(result, [sum(widths[:k]) for k in range(1, len(widths))], axis=along))


def cut_along(value, dim, count):
    before, after = (value.shape[:dim], value.shape[dim + 1 :])
    return jnp.moveaxis(value.reshape(*before, count, -1, *after), dim, 0)


def summed_on_arrival(value, axis, dim):
    pieces = cut_along(value, dim, lax.axis_size(axis))
    arrived = lax.all_to_all(pieces, axis, split_axis=0, concat_axis=0, tiled=True)
    return arrived.astype(jnp.float32).sum(axis=0)


def apply_metric(metric_root, raw_rows):
    return lax.dot_general(
        metric_root, raw_rows, (((0,), (0,)), ((), ())), preferred_element_type=jnp.float32
    ).astype(jnp.bfloat16)


def body(raw_integrals, metric_root, eps_occ, eps_vir):
    ia_count = lax.axis_size("ia")
    aux_count = lax.axis_size("aux")
    row_index = lax.axis_index("ia")
    col_index = lax.axis_index("ja")
    aux_index = lax.axis_index("aux")
    pieces = raw_integrals.shape[0]
    aux_total = metric_root.shape[0]
    narrow = V // (ia_count * aux_count)
    half_width = V // aux_count
    by_block = raw_integrals.reshape(pieces, ia_count, OB, ia_count * aux_count, narrow)
    own_rows = by_block.transpose(1, 3, 0, 2, 4).reshape(
        ia_count * ia_count * aux_count, pieces, OB * narrow
    )
    by_column = raw_integrals.reshape(pieces, ia_count, OB, ia_count, aux_count, narrow)
    own_cols = by_column.transpose(3, 1, 4, 0, 2, 5).reshape(
        ia_count * ia_count * aux_count, pieces, OB * narrow
    )
    got_rows, got_cols = sent_together((own_rows, own_cols), ("ia", "ja", "aux"), 0, 1, 2)
    joined = jnp.concatenate([got_rows[0], got_cols[0]], axis=1)
    fitted = apply_metric(metric_root, joined)
    row_block = fitted[:, : OB * narrow].reshape(aux_total, OB, narrow)
    col_block = fitted[:, OB * narrow :].reshape(aux_total, OB, narrow)
    block_i = lax.all_gather(row_block, ("ja", "aux"), axis=2, tiled=True)
    block_j = lax.all_gather(col_block, ("ia", "aux"), axis=2, tiled=True)
    half_i = lax.dynamic_slice_in_dim(block_i, aux_index * half_width, half_width, 2)
    half_j = lax.dynamic_slice_in_dim(block_j, aux_index * half_width, half_width, 2)
    flat_i = block_i.reshape(aux_total, OB * V)
    flat_j = block_j.reshape(aux_total, OB * V)
    contract_aux = (((0,), (0,)), ((), ()))
    direct_part = lax.dot_general(
        half_i.reshape(aux_total, OB * half_width),
        flat_j,
        contract_aux,
        preferred_element_type=jnp.float32,
    )
    swap_part = lax.dot_general(
        flat_i,
        half_j.reshape(aux_total, OB * half_width),
        contract_aux,
        preferred_element_type=jnp.float32,
    )
    swap_part = swap_part.reshape(OB, V, OB, half_width).transpose(0, 3, 2, 1)
    energy_i = lax.dynamic_slice_in_dim(eps_occ, row_index * OB, OB, 0)
    energy_j = lax.dynamic_slice_in_dim(eps_occ, col_index * OB, OB, 0)
    energy_a = lax.dynamic_slice_in_dim(eps_vir, aux_index * half_width, half_width, 0)
    denominator = (
        energy_a[None, :, None, None]
        + eps_vir[None, None, None, :]
        - energy_i[:, None, None, None]
        - energy_j[None, None, :, None]
    )
    amplitude = (
        (2.0 * direct_part.reshape(OB, half_width, OB, V) - swap_part) / denominator
    ).astype(jnp.bfloat16)
    amplitude = amplitude.reshape(OB * half_width, OB * V)
    ja_count = lax.axis_size("ja")
    q_rows = aux_total // ja_count
    share = summed_on_arrival(
        lax.dot_general(
            flat_j, amplitude, (((1,), (1,)), ((), ())), preferred_element_type=jnp.float32
        ).astype(jnp.bfloat16),
        "ja",
        0,
    )
    return share.reshape(q_rows, OB, half_width)


def solution(mesh):
    in_specs = (P(("ia", "ja", "aux"), None, None), P(), P(), P())
    out_specs = P("ja", "ia", "aux")
    return jax.shard_map(body, mesh=mesh, in_specs=in_specs, out_specs=out_specs, check_vma=False)
```

profile of v0, /device:TPU:1, one launch (start us, length us, event | category | flops | bytes accessed | tf_op | source)
XLA Modules:
  0.0 243.1 jit_solution(10909698681024934031)
XLA Ops:
  6.5 4.9 %reshape.89 = bf16[16,8,3,8,2,32]{5,4,3,2,1,0:T(2,128)(2,1)} reshape(bf16[16,24,512]{2,1,0:T(8,128)(2,1)} %param.4) | data formatting | bytes 786432 | tf_op jit(solution)/shard_map/reshape | solution.py:48
  11.4 2.9 %reshape.87 = bf16[16,8,3,16,32]{4,3,2,1,0:T(8,128)(2,1)} reshape(bf16[16,24,512]{2,1,0:T(8,128)(2,1)} %param.4) | data formatting | bytes 786432 | tf_op jit(solution)/shard_map/reshape | solution.py:44
  14.3 2.6 %copy.23 = bf16[16,8,3,8,2,32]{5,2,0,4,1,3:T(4,128)(2,1)S(1)} copy(bf16[16,8,3,8,2,32]{5,4,3,2,1,0:T(2,128)(2,1)} %reshape.89) | data formatting | bytes 786432 | tf_op jit(solution)/shard_map/reshape | solution.py:48
  16.9 1.0 reshape.90
  17.9 2.5 %copy.24 = bf16[16,8,3,16,32]{4,2,0,3,1:T(4,128)(2,1)S(1)} copy(bf16[16,8,3,16,32]{4,3,2,1,0:T(8,128)(2,1)} %reshape.87) | data formatting | bytes 786432 | tf_op jit(solution)/shard_map/reshape | solution.py:44
  20.4 1.0 reshape.88
  21.5 0.5 pad_maximum_fusion
  21.9 31.0 %all_to_all.17 = bf16[128,16,192]{2,1,0:T(8,128)(2,1)S(1)} all-to-all(bf16[128,16,192]{2,1,0:T(8,128)(2,1)S(1)} %pad_maximum_fusion), channel_id=1, replica_groups=mesh['ia'=8,'ja'=8,'aux'=2] {'ia','ja','aux'}, dimensions={0} | all-to-all | bytes 1572864 | tf_op jit(solution)/shard_map/all_to_all | solution.py:13
  52.9 0.3 slice_bitcast_fusion.1
  53.2 5.3 %fusion.14 = bf16[2048,192]{0,1:T(8,128)(2,1)S(1)} fusion(bf16[2048,2048]{1,0:T(8,128)(2,1)} %param.5, bf16[2048,96]{1,0:T(8,128)(2,1)S(1)} %get-tuple-element.6, bf16[2048,96]{1,0:T(8,128)(2,1)S(1)} %get-tuple-element.5), kind=kOutput, calls=%fused_computation.14 | convolution fusion | flops 1612578816 | bytes 9961472 | tf_op jit(solution)/shard_map/dot_general | solution.py:29
  58.5 1.0 fusion.21
  59.7 0.5 all-gather.5.cloned.1.call-update
  60.5 0.3 broadcast_subtract_fusion
  60.8 55.6 %all-gather.3.cloned.1.call-done = bf16[2048,3,512]{0,2,1:T(8,128)(2,1)} async-done(((bf16[2048,3,32]{0,2,1:T(8,128)(2,1)}), bf16[2048,3,512]{0,2,1:T(8,128)(2,1)}) %all-gather.3.cloned.1.call-update) | async-done | bytes 6291472 | tf_op jit(solution)/shard_map/all_gather | solution.py:58
  116.4 53.9 %all-gather.5.cloned.1.call-done = bf16[2048,3,512]{0,2,1:T(8,128)(2,1)} async-done(((bf16[2048,3,32]{0,2,1:T(8,128)(2,1)}), bf16[2048,3,512]{0,2,1:T(8,128)(2,1)}) %all-gather.5.cloned.1.call-update) | async-done | bytes 6291472 | tf_op jit(solution)/shard_map/all_gather | solution.py:57
  170.3 8.4 %fusion = f32[3,512,3,256]{1,3,2,0:T(8,128)S(1)} fusion(bf16[2048,3,512]{0,2,1:T(8,128)(2,1)} %all-gather.5.cloned.1.call-done, bf16[2048,3,512]{0,2,1:T(8,128)(2,1)} %all-gather.3.cloned.1.call-done, s32[]{:T(128)S(6)} %select_n.11), kind=kOutput, calls=%fused_computation | convolution fusion | flops 4831838208 | bytes 14155780 | tf_op jit(solution)/shard_map/dot_general | solution.py:70
  178.8 5.6 %fusion.5 = bf16[3,256,3,512]{3,1,2,0:T(8,128)(2,1)S(1)} fusion(f32[3,512,3,256]{1,3,2,0:T(8,128)S(1)} %fusion, bf16[2048,3,512]{0,2,1:T(8,128)(2,1)S(1)} %copy-done.2, bf16[2048,3,512]{0,2,1:T(8,128)(2,1)S(1)} %copy-done.3, s32[]{:T(128)S(6)} %select_n.11, f32[3]{0:T(128)S(1)} %get-tuple-element.10, f32[3,256,512]{2,1,0:T(8,128)S(1)} %broadcast_subtract_fusion), kind=kOutput, calls=%fused_computation.7 | convolution fusion | flops 4837736448 | bytes 18088452 | tf_op jit(solution)/shard_map/dot_general | solution.py:64
  184.4 2.0 copy.14
  186.4 0.8 copy.20
  187.2 5.4 %convolution_convert_fusion = bf16[2048,768]{1,0:T(8,128)(2,1)S(1)} fusion(bf16[2048,1536]{0,1:T(8,128)(2,1)S(1)} %bitcast.82, bf16[768,1536]{1,0:T(8,128)(2,1)S(1)} %bitcast.79), kind=kOutput, calls=%fused_computation.8 | convolution fusion | flops 4833411072 | bytes 11796480 | tf_op jit(solution)/shard_map/dot_general | solution.py:93
  192.6 41.8 %all_to_all.18 = bf16[8,256,768]{2,1,0:T(8,128)(2,1)S(1)} all-to-all(bf16[8,256,768]{2,1,0:T(8,128)(2,1)S(1)} %bitcast.77), channel_id=1, replica_groups=mesh['ia'=8,'ja'=8,'aux'=2] {'ja'}, dimensions={0} | all-to-all | bytes 6291456 | tf_op jit(solution)/shard_map/all_to_all | solution.py:24
  234.4 0.4 convert_reduce_fusion
  234.8 0.3 copy.15
  235.1 1.1 copy.16
  (14 shorter events, 0.5 us)
Async XLA Ops:
  6.5 109.9 %all-gather.3.cloned.1.call-start = ((), (), s32[]{:S(2)}) async-start(), calls=%async_computation.2 | async-start | bytes 6684672 | tf_op jit(solution)/shard_map/all_gather | solution.py:58
  53.1 7.1 %copy-start = (f32[512]{0:T(512)S(1)}, f32[512]{0:T(512)}, u32[]{:S(2)}) copy-start(f32[512]{0:T(512)} %param.7) | copy-start | bytes 6148
  53.1 7.2 %copy-start.1 = (f32[24]{0:T(128)S(1)}, f32[24]{0:T(128)}, u32[]{:S(2)}) copy-start(f32[24]{0:T(128)} %param.6) | copy-start | bytes 292
  59.5 110.8 %all-gather.5.cloned.1.call-start = ((), (), s32[]{:S(2)}) async-start(), calls=%async_computation.3 | async-start | bytes 6684672 | tf_op jit(solution)/shard_map/all_gather | solution.py:57
  170.3 8.5 %copy-start.2 = (bf16[2048,3,512]{0,2,1:T(8,128)(2,1)S(1)}, bf16[2048,3,512]{0,2,1:T(8,128)(2,1)}, u32[]{:S(2)}) copy-start(bf16[2048,3,512]{0,2,1:T(8,128)(2,1)} %all-gather.3.cloned.1.call-done) | copy-start | bytes 18874372
  170.3 8.5 %copy-start.3 = (bf16[2048,3,512]{0,2,1:T(8,128)(2,1)S(1)}, bf16[2048,3,512]{0,2,1:T(8,128)(2,1)}, u32[]{:S(2)}) copy-start(bf16[2048,3,512]{0,2,1:T(8,128)(2,1)} %all-gather.5.cloned.1.call-done) | copy-start | bytes 18874372
Sparse Core Ops, SparseCore 0:
  59.6 56.7 all-gather.2
  118.1 52.1 all-gather.4
where the time goes:
time: 243 us
  waiting for transfers between devices  110 us (45%)
  blocking collectives  72.7 us (30%)
  matrix products  24.8 us (10%)
  local copies, waits for them, and re-layouts  20.5 us (8%)
  between operations  13.6 us (6%)
    all_gather x1, waiting for transfers between devices, body(): block_j = lax.all_gather(col_block, ('ia', 'aux'), axis=2, tiled=True)  55.6 us
    all_gather x1, waiting for transfers between devices, body(): block_i = lax.all_gather(row_block, ('ja', 'aux'), axis=2, tiled=True)  53.9 us
    all_to_all x1, blocking collectives, summed_on_arrival(): lax.all_to_all(pieces, axis, split_axis=0, concat_axis=0, tiled=True)  41.8 us
    all_to_all x1, blocking collectives, sent_together(): lax.all_to_all(both, axis, split_axis=split_dim, concat_axis=concat_dim,...  31 us
    dot_general x1, matrix products, body(): lax.dot_general(flat_i, half_j.reshape(aux_total, OB * half_width), contr...  8.44 us
    reshape x2, local copies, waits for them, and re-layouts, body(): raw_integrals.reshape(pieces, ia_count, OB, ia_count, aux_count, narrow)  7.46 us
    dot_general x1, matrix products, body(): lax.dot_general(half_i.reshape(aux_total, OB * half_width), flat_j, contr...  5.6 us
    dot_general x1, matrix products, body(): lax.dot_general(flat_j, amplitude, (((1,), (1,)), ((), ())), preferred_el...  5.41 us
  transfers between devices with their start and end apart: 2, of which 2 were waited for; matrix products, arithmetic and copies ran while one was open for 0% of the time, Pallas kernels for 0%

commit v1 on v0

v1 whole, which is shorter than its diff:
```python
import functools

import jax
import jax.numpy as jnp
from jax import lax
from jax.experimental import pallas as pl
from jax.experimental.pallas import tpu as pltpu
from jax.sharding import PartitionSpec as P

OB = 3
V = 512
NC = 4
QC = 512
LA = 256
HALF = 256
ROWS = OB * HALF
F32 = jnp.float32
BF16 = jnp.bfloat16
MESH = pl.DeviceIdType.MESH


def kernel(
    got_ref, met_hbm, eocc_ref, evr_ref, evc_ref, out_ref,
    fi, fj, met, acc, amp, gown, sib_s, sib_r, opp_s, opp_r, rs_s, rs_r,
    met_sem, ss, rs, gs, gr,
):
    ia = lax.axis_index("ia")
    ja = lax.axis_index("ja")
    aux = lax.axis_index("aux")
    z, yh = lax.div(ia, 2), lax.rem(ia, 2)
    x, core = lax.div(ja, 2), lax.rem(ja, 2)
    y = yh * 2 + aux

    def step(v, d):
        return lax.rem(v + (d + 4), 4)

    def ydev(d):
        w = step(y, d)
        return {"ia": z * 2 + lax.div(w, 2), "ja": ja, "aux": lax.rem(w, 2)}

    def zdev(d):
        return {"ia": step(z, d) * 2 + yh, "ja": ja, "aux": aux}

    def xdev(d):
        return {"ia": ia, "ja": step(x, d) * 2 + core, "aux": aux}

    sib = {"ia": ia, "ja": x * 2 + (1 - core), "aux": aux}
    ypart = {"ia": ia, "ja": ja, "aux": 1 - aux}

    met_copies = [
        pltpu.make_async_copy(met_hbm.at[:, pl.ds(c * QC, QC)], met.at[c], met_sem.at[c])
        for c in range(NC)
    ]
    for c in range(NC):
        met_copies[c].start()

    barrier = pltpu.get_barrier_semaphore()
    for dev in (ydev(1), ydev(-1), zdev(1), zdev(-1), xdev(1), xdev(-1), sib):
        pl.semaphore_signal(barrier, inc=1, device_id=dev, device_id_type=MESH)
    pl.semaphore_wait(barrier, 7)

    pending = []

    def put(ref, c, n, dev):
        copy = pltpu.make_async_remote_copy(
            src_ref=ref, dst_ref=ref, send_sem=ss.at[c, n], recv_sem=rs.at[c, n],
            device_id=dev, device_id_type=MESH,
        )
        copy.start()
        pending.append(copy)

    def arrived(ref, c, n):
        pltpu.make_async_remote_copy(
            src_ref=ref, dst_ref=ref, send_sem=ss.at[c, n], recv_sem=rs.at[c, n],
            device_id=sib, device_id_type=MESH,
        ).wait_recv()

    def fja(c, zz, yy, r=slice(None)):
        return fj.at[c, :, zz, yy, r, pl.ds(0, LA)]

    def fjb(c, zz, yy, r=slice(None)):
        return fj.at[c, :, zz, yy, r, pl.ds(LA, QC - LA)]

    lo, hi = pl.ds(0, 16), pl.ds(16, 16)
    first2, last2 = pl.ds(0, 2), pl.ds(2, 2)
    every = slice(None)
    yp, ym, y2 = step(y, 1), step(y, -1), step(y, 2)
    zp, zm, z2 = step(z, 1), step(z, -1), step(z, 2)
    xp, xm, x2 = step(x, 1), step(x, -1), step(x, 2)

    def fit(c):
        met_copies[c].wait()
        r = lax.dot_general(
            got_ref[...], met[c], (((0,), (0,)), ((), ())), preferred_element_type=F32
        ).astype(BF16)
        for k in range(OB):
            fi[c, k, x, core, aux] = r[32 * k : 32 * k + 32]
            fj[c, k, z, y] = r[128 + 32 * k : 160 + 32 * k]

    def p0(c):
        put(fja(c, z, y), c, 0, ydev(1))
        put(fja(c, z, y), c, 1, ydev(-1))
        put(fjb(c, z, y), c, 2, zdev(1))
        put(fjb(c, z, y), c, 3, zdev(-1))
        put(fi.at[c, :, x, core, aux], c, 4, ypart)

    def p1(c):
        arrived(fi.at[c, :, x, core, 1 - aux], c, 4)
        put(fi.at[c, :, x, core], c, 9, xdev(1))
        put(fi.at[c, :, x, core], c, 10, xdev(-1))
        put(fi.at[c, :, x, core], c, 11, sib)
        arrived(fja(c, z, ym), c, 0)
        put(fja(c, z, ym, lo), c, 5, ydev(1))
        arrived(fja(c, z, yp), c, 1)
        put(fja(c, z, yp, hi), c, 6, ydev(-1))
        arrived(fjb(c, zm, y), c, 2)
        put(fjb(c, zm, y, lo), c, 7, zdev(1))
        arrived(fjb(c, zp, y), c, 3)
        put(fjb(c, zp, y, hi), c, 8, zdev(-1))

    def p2(c):
        arrived(fja(c, z, y2, lo), c, 5)
        arrived(fja(c, z, y2, hi), c, 6)
        put(fja(c, z, every), c, 12, zdev(1))
        put(fja(c, z, every), c, 13, zdev(-1))
        arrived(fjb(c, z2, y, lo), c, 7)
        arrived(fjb(c, z2, y, hi), c, 8)
        put(fjb(c, every, y), c, 14, ydev(1))
        put(fjb(c, every, y), c, 15, ydev(-1))
        arrived(fi.at[c, :, xm, core], c, 9)
        put(fi.at[c, :, xm, core, 0], c, 16, xdev(1))
        put(fi.at[c, :, xm, core], c, 17, sib)
        arrived(fi.at[c, :, xp, core], c, 10)
        put(fi.at[c, :, xp, core, 1], c, 18, xdev(-1))
        put(fi.at[c, :, xp, core], c, 19, sib)

    def p3(c):
        arrived(fja(c, zm, every), c, 12)
        put(fja(c, zm, first2), c, 20, zdev(1))
        arrived(fja(c, zp, every), c, 13)
        put(fja(c, zp, last2), c, 21, zdev(-1))
        arrived(fjb(c, every, ym), c, 14)
        put(fjb(c, first2, ym), c, 22, ydev(1))
        arrived(fjb(c, every, yp), c, 15)
        put(fjb(c, last2, yp), c, 23, ydev(-1))
        arrived(fi.at[c, :, x2, core, 0], c, 16)
        arrived(fi.at[c, :, x2, core, 1], c, 18)
        put(fi.at[c, :, x2, core], c, 24, sib)

    def p4(c):
        arrived(fja(c, z2, first2), c, 20)
        arrived(fja(c, z2, last2), c, 21)
        arrived(fjb(c, first2, y2), c, 22)
        arrived(fjb(c, last2, y2), c, 23)
        other = 1 - core
        arrived(fi.at[c, :, x, other], c, 11)
        arrived(fi.at[c, :, xm, other], c, 17)
        arrived(fi.at[c, :, xp, other], c, 19)
        arrived(fi.at[c, :, x2, other], c, 24)

    over_q = (((1,), (1,)), ((), ()))

    def coulomb(c):
        def direct(l, carry):
            part = lax.dot_general(
                fi[c, :, pl.ds(2 * aux, 2)].reshape(ROWS, QC),
                fj[c, l].reshape(V, QC),
                over_q,
                preferred_element_type=F32,
            )
            for k in range(OB):
                term = 2.0 * part[k * HALF : (k + 1) * HALF]
                acc[k, l] = term if c == 0 else acc[k, l] + term
            return carry

        def swap(k, carry):
            part = lax.dot_general(
                fj[c, :, pl.ds(2 * aux, 2)].reshape(ROWS, QC),
                fi[c, k].reshape(V, QC),
                over_q,
                preferred_element_type=F32,
            )
            for l in range(OB):
                acc[k, l] = acc[k, l] - part[l * HALF : (l + 1) * HALF]
            return carry

        lax.fori_loop(0, OB, direct, 0)
        lax.fori_loop(0, OB, swap, 0)

    fit(0)
    p0(0)
    fit(1)
    p0(1)
    p1(0)
    fit(2)
    p0(2)
    p1(1)
    p2(0)
    fit(3)
    p0(3)
    p1(2)
    p2(1)
    p1(3)
    p3(0)
    p2(2)
    p4(0)
    coulomb(0)
    p3(1)
    p2(3)
    p4(1)
    coulomb(1)
    p3(2)
    p4(2)
    p3(3)
    coulomb(2)
    p4(3)
    coulomb(3)

    for k in range(OB):
        for l in range(OB):
            den = evc_ref[...] + evr_ref[...] - eocc_ref[OB * ia + k] - eocc_ref[OB * ja + l]
            amp[k, :, l * V : (l + 1) * V] = (acc[k, l] / den).astype(BF16)

    def partial(block, half):
        lanes = pl.ds(pl.multiple_of(half * HALF, HALF), HALF)
        total = None
        for l in range(OB):
            term = jnp.dot(
                amp[:, :, l * V : (l + 1) * V].reshape(ROWS, V),
                fj[block, l, :, :, :, lanes].reshape(V, HALF),
                preferred_element_type=F32,
            )
            total = term if total is None else total + term
        return total

    def send(src, dst, n, dev):
        copy = pltpu.make_async_remote_copy(
            src_ref=src, dst_ref=dst, send_sem=gs.at[n], recv_sem=gr.at[n],
            device_id=dev, device_id_type=MESH,
        )
        copy.start()
        pending.append(copy)

    def landed(dst, n):
        pltpu.make_async_remote_copy(
            src_ref=dst, dst_ref=dst, send_sem=gs.at[n], recv_sem=gr.at[n],
            device_id=sib, device_id_type=MESH,
        ).wait_recv()

    H = ROWS // 2
    top, bottom = pl.ds(0, H), pl.ds(H, H)

    def both_cores(m, block):
        sib_s[m] = partial(block, 1 - core).astype(BF16)
        send(sib_s.at[m], sib_r.at[m], m, sib)
        gown[m] = partial(block, core)

    both_cores(0, x2)
    both_cores(1, xp)
    landed(sib_r.at[0], 0)
    opp_s[...] = (gown[0] + sib_r[0].astype(F32)).astype(BF16)
    send(opp_s.at[top], opp_r.at[top], 4, xdev(1))
    send(opp_s.at[bottom], opp_r.at[bottom], 5, xdev(-1))
    both_cores(2, xm)
    landed(sib_r.at[1], 1)
    rs_s[0, bottom] = (gown[1, bottom] + sib_r[1, bottom].astype(F32)).astype(BF16)
    send(rs_s.at[0, bottom], rs_r.at[0, bottom], 6, xdev(1))
    both_cores(3, x)
    landed(sib_r.at[2], 2)
    rs_s[1, top] = (gown[2, top] + sib_r[2, top].astype(F32)).astype(BF16)
    send(rs_s.at[1, top], rs_r.at[1, top], 7, xdev(-1))
    landed(opp_r.at[top], 4)
    rs_s[0, top] = (
        gown[1, top] + sib_r[1, top].astype(F32) + opp_r[top].astype(F32)
    ).astype(BF16)
    send(rs_s.at[0, top], rs_r.at[0, top], 8, xdev(1))
    landed(opp_r.at[bottom], 5)
    rs_s[1, bottom] = (
        gown[2, bottom] + sib_r[2, bottom].astype(F32) + opp_r[bottom].astype(F32)
    ).astype(BF16)
    send(rs_s.at[1, bottom], rs_r.at[1, bottom], 9, xdev(-1))
    landed(sib_r.at[3], 3)
    landed(rs_r.at[0, bottom], 6)
    landed(rs_r.at[1, top], 7)
    landed(rs_r.at[0, top], 8)
    landed(rs_r.at[1, bottom], 9)
    for k in range(OB):
        r = slice(k * HALF, (k + 1) * HALF)
        total = (
            gown[3, r]
            + sib_r[3, r].astype(F32)
            + rs_r[0, r].astype(F32)
            + rs_r[1, r].astype(F32)
        )
        out_ref[k] = total.T
    for copy in pending:
        copy.wait_send()


def body(raw_integrals, metric_root, eps_occ, eps_vir):
    aux_index = lax.axis_index("aux")
    pieces = raw_integrals.shape[0]
    aux_total = metric_root.shape[0]
    narrow = V // 16
    by_slice = raw_integrals.reshape(pieces, 8, OB, 16, narrow)
    blocks = by_slice.transpose(1, 3, 0, 2, 4).reshape(8, 8, 2, pieces, OB * narrow)
    blocks = jnp.pad(blocks, ((0, 0),) * 4 + ((0, 128 - OB * narrow),))
    both = jnp.concatenate([blocks, blocks.transpose(1, 0, 2, 3, 4)], axis=4).reshape(128, pieces, 256)
    got = lax.all_to_all(both, ("ia", "ja", "aux"), split_axis=0, concat_axis=0, tiled=True)
    got = got.reshape(aux_total, 256)
    ev_half = lax.dynamic_slice_in_dim(eps_vir, aux_index * HALF, HALF, 0)
    vmem = pl.BlockSpec(memory_space=pltpu.VMEM)
    out = pl.pallas_call(
        kernel,
        out_shape=jax.ShapeDtypeStruct((OB, HALF, HALF), F32),
        in_specs=[
            vmem,
            pl.BlockSpec(memory_space=pl.ANY),
            pl.BlockSpec(memory_space=pltpu.SMEM),
            vmem,
            vmem,
        ],
        out_specs=vmem,
        scratch_shapes=[
            pltpu.VMEM((NC, OB, 4, 2, 2, 32, QC), BF16),
            pltpu.VMEM((NC, OB, 4, 4, 32, QC), BF16),
            pltpu.VMEM((NC, aux_total, QC), BF16),
            pltpu.VMEM((OB, OB, HALF, V), F32),
            pltpu.VMEM((OB, HALF, OB * V), BF16),
            pltpu.VMEM((4, ROWS, HALF), F32),
            pltpu.VMEM((4, ROWS, HALF), BF16),
            pltpu.VMEM((4, ROWS, HALF), BF16),
            pltpu.VMEM((ROWS, HALF), BF16),
            pltpu.VMEM((ROWS, HALF), BF16),
            pltpu.VMEM((2, ROWS, HALF), BF16),
            pltpu.VMEM((2, ROWS, HALF), BF16),
            pltpu.SemaphoreType.DMA((NC,)),
            pltpu.SemaphoreType.DMA((NC, 25)),
            pltpu.SemaphoreType.DMA((NC, 25)),
            pltpu.SemaphoreType.DMA((10,)),
            pltpu.SemaphoreType.DMA((10,)),
        ],
        compiler_params=pltpu.CompilerParams(
            collective_id=0, has_side_effects=True, vmem_limit_bytes=60 * 2**20
        ),
    )(got, metric_root, eps_occ, eps_vir.reshape(1, V), ev_half.reshape(HALF, 1))
    return out.transpose(1, 0, 2)


def solution(mesh):
    in_specs = (P(("ia", "ja", "aux"), None, None), P(), P(), P())
    out_specs = P("ja", "ia", "aux")
    return jax.shard_map(body, mesh=mesh, in_specs=in_specs, out_specs=out_specs, check_vma=False)
```

time: 243 us -> 119 us (0.49)
  waiting for transfers between devices: 110 us -> 18.8 us
  Pallas kernels: 0 us -> 76.3 us
  blocking collectives: 72.7 us -> 0 us
  matrix products: 24.8 us -> 0 us
  between operations: 13.6 us -> 0.07 us
  starting transfers between devices: 0.22 us -> 11.5 us
  local copies, waits for them, and re-layouts: 20.5 us -> 10.6 us
    all_gather x2 -> x0, waiting for transfers between devices: 110 us -> none  [the longest x1 55.6 us: body(): block_j = lax.all_gather(col_block, ('ia', 'aux'), axis=2, tiled=True)]
    pallas_call x0 -> x1, Pallas kernels: none -> 76.3 us  [body(): pl.pallas_call(kernel, out_shape=jax.ShapeDtypeStruct((OB, HALF, HALF), F...]
    all_to_all x2 -> x0, blocking collectives: 72.7 us -> none  [the longest x1 41.8 us: summed_on_arrival(): lax.all_to_all(pieces, axis, split_axis=0, concat_axis=0, tiled=True)]
    dot_general x4 -> x0, matrix products: 24.8 us -> none  [the longest x1 8.44 us: body(): lax.dot_general(flat_i, half_j.reshape(aux_total, OB * half_width), contr...]
    all_to_all x0 -> x1, waiting for transfers between devices: none -> 18.8 us  [body(): lax.all_to_all(both, ('ia', 'ja', 'aux'), split_axis=0, concat_axis=0, ti...]
    all_to_all x0 -> x1, starting transfers between devices: none -> 11.5 us  [body(): lax.all_to_all(both, ('ia', 'ja', 'aux'), split_axis=0, concat_axis=0, ti...]
    reshape x7 -> x4, local copies, waits for them, and re-layouts: 16 us -> 7.21 us  [the longest x2 5.39 us: body(): by_slice = raw_integrals.reshape(pieces, 8, OB, 16, narrow)]
  transfers between devices with their start and end apart: 2 -> 1, of which waited for: 2 -> 1; matrix products, arithmetic and copies ran while one was open for 0% -> 1% of each run, Pallas kernels for 0% -> 0%
where the time goes in v1:
time: 119 us; the launch traced here: 118 us
  Pallas kernels  76.3 us (64%)
  waiting for transfers between devices  18.8 us (16%)
  starting transfers between devices  11.5 us (10%)
  local copies, waits for them, and re-layouts  10.6 us (9%)
    pallas_call x1, Pallas kernels, body(): pl.pallas_call(kernel, out_shape=jax.ShapeDtypeStruct((OB, HALF, HALF), F...  76.3 us
    all_to_all x1, waiting for transfers between devices, body(): lax.all_to_all(both, ('ia', 'ja', 'aux'), split_axis=0, concat_axis=0, ti...  18.8 us
    all_to_all x1, starting transfers between devices, body(): lax.all_to_all(both, ('ia', 'ja', 'aux'), split_axis=0, concat_axis=0, ti...  11.5 us
    reshape x2, local copies, waits for them, and re-layouts, body(): by_slice = raw_integrals.reshape(pieces, 8, OB, 16, narrow)  5.39 us
    unnamed x5, local copies, waits for them, and re-layouts  3.04 us
  transfers between devices with their start and end apart: 1, of which 1 were waited for; matrix products, arithmetic and copies ran while one was open for 1% of the time, Pallas kernels for 0%

profile of v1, /device:TPU:1, one launch (start us, length us, event | category | flops | bytes accessed | tf_op | source)
XLA Modules:
  0.0 118.3 jit_solution(10565845465937164569)
XLA Ops:
  0.0 2.9 %reshape.18 = bf16[16,8,3,16,32]{4,3,2,1,0:T(8,128)(2,1)} reshape(bf16[16,24,512]{2,1,0:T(8,128)(2,1)} %param.4) | data formatting | bytes 786432 | tf_op jit(solution)/shard_map/reshape | solution.py:305
  2.9 2.5 %copy.11 = bf16[16,8,3,16,32]{4,2,0,3,1:T(4,128)(2,1)S(1)} copy(bf16[16,8,3,16,32]{4,3,2,1,0:T(8,128)(2,1)} %reshape.18) | data formatting | bytes 786432 | tf_op jit(solution)/shard_map/reshape | solution.py:305
  5.4 1.0 reshape.19
  6.4 0.1 copy_bitcast_fusion.1
  6.5 0.1 pad.4
  6.7 0.0 copy-start.1
  6.7 1.1 pad_maximum_fusion
  7.8 11.5 %all-to-all-start = ((bf16[128,16,256]{2,1,0:T(8,128)(2,1)}), bf16[128,16,256]{2,1,0:T(8,128)(2,1)S(1)}, u32[]{:S(2)}, u32[]{:S(2)}) async-start(bf16[128,16,256]{2,1,0:T(8,128)(2,1)} %bitcast.2), calls=%async_computation | async-start | bytes 2097152 | tf_op jit(solution)/shard_map/all_to_all | solution.py:309
  19.3 0.0 copy-done.1
  19.3 0.1 dynamic_slice.3
  19.4 0.8 copy.8.evc_ref
  20.2 18.8 %all-to-all-done = bf16[128,16,256]{2,1,0:T(8,128)(2,1)S(1)} async-done(((bf16[128,16,256]{2,1,0:T(8,128)(2,1)}), bf16[128,16,256]{2,1,0:T(8,128)(2,1)S(1)}, u32[]{:S(2)}, u32[]{:S(2)}) %all-to-all-start) | async-done | bytes 1048608 | tf_op jit(solution)/shard_map/all_to_all | solution.py:309
  39.0 0.0 copy-start
  39.0 1.0 copy-done
  39.9 76.3 %shard_map.46 = f32[3,256,256]{2,1,0:T(8,128)} custom-call(bf16[2048,256]{1,0:T(8,128)(2,1)} %bitcast.11, bf16[2048,2048]{1,0:T(8,128)(2,1)} %met_hbm.1, f32[24]{0:T(128)} %eocc_ref.1, f32[1,512]{1,0:T(1,128)} %bitcast.13, f32[256,1]{1,0:T(8,128)} %copy.8.evc_ref), custom_call_target="tpu_custom_call" | custom-call | tf_op jit(solution)/shard_map/pallas_call | solution.py:313
  116.3 2.1 %copy.13 = f32[256,3,256]{2,0,1:T(8,128)} copy(f32[256,3,256]{2,0,1:T(8,128)} %bitcast.12) | data formatting | bytes 1572864
Async XLA Ops:
  6.7 12.6 %copy-start.1 = (f32[512]{0:T(512)S(1)}, f32[512]{0:T(512)}, u32[]{:S(2)}) copy-start(f32[512]{0:T(512)} %param.7) | copy-start | bytes 6148
  7.8 31.2 %all-to-all-start = ((bf16[128,16,256]{2,1,0:T(8,128)(2,1)}), bf16[128,16,256]{2,1,0:T(8,128)(2,1)S(1)}, u32[]{:S(2)}, u32[]{:S(2)}) async-start(bf16[128,16,256]{2,1,0:T(8,128)(2,1)} %bitcast.2), calls=%async_computation | async-start | bytes 2097152 | tf_op jit(solution)/shard_map/all_to_all | solution.py:309
  39.0 1.0 copy-start

commit v2 on v1

--- a/solution.py
+++ b/solution.py
@@ -297,17 +297,75 @@
         copy.wait_send()
 
 
+def spread_kernel(raw_ref, got_ref, send, own_sem, send_sem, recv_sem):
+    ia = lax.axis_index("ia")
+    ja = lax.axis_index("ja")
+    aux = lax.axis_index("aux")
+    me = ia * 16 + ja * 2 + aux
+    pieces = raw_ref.shape[0]
+    occ = raw_ref.shape[1]
+    n = pieces * occ
+    row = lax.broadcasted_iota(jnp.int32, (n, n), 0)
+    col = lax.broadcasted_iota(jnp.int32, (n, n), 1)
+    pick = ((row & 15) * occ + (row >> 4) == col).astype(F32).astype(BF16)
+    by_occ = jnp.dot(pick, raw_ref[...].reshape(n, V), preferred_element_type=F32)
+    lane = lax.broadcasted_iota(jnp.int32, (pieces, 128), 1)
+    for t in range(8):
+        for tile in range(4):
+            rows = [
+                by_occ[(OB * t + k) * 16 : (OB * t + k) * 16 + 16, tile * 128 : tile * 128 + 128]
+                for k in range(OB)
+            ]
+            for q in range(4):
+                moved = [
+                    r if k == q else pltpu.roll(r, (32 * (k - q)) % 128, 1)
+                    for k, r in enumerate(rows)
+                ]
+                block = jnp.where(lane < 32, moved[0], jnp.where(lane < 64, moved[1], jnp.where(lane < 96, moved[2], 0.0))).astype(BF16)
+                s = tile * 4 + q
+                send[t * 16 + s, :, 0:128] = block
+                send[(s // 2) * 16 + t * 2 + s % 2, :, 128:256] = block
+    mine = got_ref.at[pl.ds(me * 16, 16)]
+    own = pltpu.make_async_copy(send.at[me], mine, recv_sem)
+    own.start()
+    z, y, x, core = ia >> 1, (ia & 1) * 2 + aux, ja >> 1, ja & 1
+
+    def one(step_, carry):
+        o = (step_ * 37) & 127
+        dz = (z + (o >> 5)) & 3
+        dy = (y + (o >> 3)) & 3
+        dx = (x + (o >> 1)) & 3
+        dc = (core + o) & 1
+        tia, tja, taux = dz * 2 + (dy >> 1), dx * 2 + dc, dy & 1
+        pltpu.make_async_remote_copy(
+            src_ref=send.at[tia * 16 + tja * 2 + taux], dst_ref=mine,
+            send_sem=send_sem, recv_sem=recv_sem,
+            device_id={"ia": tia, "ja": tja, "aux": taux}, device_id_type=MESH,
+        ).start()
+        return carry
+
+    lax.fori_loop(1, 128, one, 0)
+    pltpu.make_async_copy(send, send, recv_sem).wait()
+    pltpu.make_async_copy(send.at[pl.ds(0, 127)], send.at[pl.ds(0, 127)], send_sem).wait()
+
+
 def body(raw_integrals, metric_root, eps_occ, eps_vir):
     aux_index = lax.axis_index("aux")
     pieces = raw_integrals.shape[0]
     aux_total = metric_root.shape[0]
-    narrow = V // 16
-    by_slice = raw_integrals.reshape(pieces, 8, OB, 16, narrow)
-    blocks = by_slice.transpose(1, 3, 0, 2, 4).reshape(8, 8, 2, pieces, OB * narrow)
-    blocks = jnp.pad(blocks, ((0, 0),) * 4 + ((0, 128 - OB * narrow),))
-    both = jnp.concatenate([blocks, blocks.transpose(1, 0, 2, 3, 4)], axis=4).reshape(128, pieces, 256)
-    got = lax.all_to_all(both, ("ia", "ja", "aux"), split_axis=0, concat_axis=0, tiled=True)
-    got = got.reshape(aux_total, 256)
+    got = pl.pallas_call(
+        spread_kernel,
+        out_shape=jax.ShapeDtypeStruct((aux_total, 256), BF16),
+        in_specs=[pl.BlockSpec(memory_space=pltpu.VMEM)],
+        out_specs=pl.BlockSpec(memory_space=pltpu.VMEM),
+        scratch_shapes=[
+            pltpu.VMEM((128, pieces, 256), BF16),
+            pltpu.SemaphoreType.DMA,
+            pltpu.SemaphoreType.DMA,
+            pltpu.SemaphoreType.DMA,
+        ],
+        compiler_params=pltpu.CompilerParams(has_side_effects=True),
+    )(raw_integrals)
     ev_half = lax.dynamic_slice_in_dim(eps_vir, aux_index * HALF, HALF, 0)
     vmem = pl.BlockSpec(memory_space=pltpu.VMEM)
     out = pl.pallas_call(

time: 119 us -> 114 us (0.958)
  Pallas kernels: 76.3 us -> 110 us
  waiting for transfers between devices: 18.8 us -> 0 us
  starting transfers between devices: 11.5 us -> 0 us
  local copies, waits for them, and re-layouts: 10.6 us -> 3.62 us
    pallas_call x0 -> x1, Pallas kernels: none -> 33.1 us  [body(): pl.pallas_call(spread_kernel, out_shape=jax.ShapeDtypeStruct((aux_total,...]
    all_to_all x1 -> x0, waiting for transfers between devices: 18.8 us -> none  [body(): lax.all_to_all(both, ('ia', 'ja', 'aux'), split_axis=0, concat_axis=0, ti...]
    all_to_all x1 -> x0, starting transfers between devices: 11.5 us -> none  [body(): lax.all_to_all(both, ('ia', 'ja', 'aux'), split_axis=0, concat_axis=0, ti...]
    reshape x3 -> x0, local copies, waits for them, and re-layouts: 6.4 us -> none  [the longest x2 5.39 us: body(): by_slice = raw_integrals.reshape(pieces, 8, OB, 16, narrow)]
    unnamed x5 -> x1, local copies, waits for them, and re-layouts: 3.04 us -> 2.06 us
  transfers between devices with their start and end apart: 1 -> 0, of which waited for: 1 -> 0; matrix products, arithmetic and copies ran while one was open for 1% -> 0% of each run, Pallas kernels for 0% -> 0%
where the time goes in v2:
time: 114 us; the launch traced here: 113 us
  Pallas kernels  110 us (96%)
  local copies, waits for them, and re-layouts  3.62 us (3%)
    pallas_call x1, Pallas kernels, body(): pl.pallas_call(kernel, out_shape=jax.ShapeDtypeStruct((OB, HALF, HALF), F...  76.6 us
    pallas_call x1, Pallas kernels, body(): pl.pallas_call(spread_kernel, out_shape=jax.ShapeDtypeStruct((aux_total,...  33.1 us

profile of v2, /device:TPU:1, one launch (start us, length us, event | category | flops | bytes accessed | tf_op | source)
XLA Modules:
  0.0 113.3 jit_solution(8843572611751638335)
XLA Ops:
  0.0 0.8 dynamic_slice.3
  0.8 0.8 copy.5.evc_ref
  1.6 33.1 %shard_map.46.got_ref = bf16[2048,256]{1,0:T(8,128)(2,1)} custom-call(bf16[16,24,512]{2,1,0:T(8,128)(2,1)} %raw_ref.1), custom_call_target="tpu_custom_call" | custom-call | tf_op jit(solution)/shard_map/pallas_call | solution.py:356
  34.6 76.6 %shard_map.47 = f32[3,256,256]{2,1,0:T(8,128)} custom-call(bf16[2048,256]{1,0:T(8,128)(2,1)} %shard_map.46.got_ref, bf16[2048,2048]{1,0:T(8,128)(2,1)} %met_hbm.1, f32[24]{0:T(128)} %eocc_ref.1, f32[1,512]{1,0:T(1,128)} %bitcast.4, f32[256,1]{1,0:T(8,128)} %copy.5.evc_ref), custom_call_target="tpu_custom_call" | custom-call | tf_op jit(solution)/shard_map/pallas_call | solution.py:371
  111.3 2.1 %copy.7 = f32[256,3,256]{2,0,1:T(8,128)} copy(f32[256,3,256]{2,0,1:T(8,128)} %bitcast.3) | data formatting | bytes 1572864

commit v3 on v0

v3 whole, which is shorter than its diff:
```python
import jax
import jax.numpy as jnp
from jax import lax
from jax.experimental import pallas as pl
from jax.experimental.pallas import tpu as pltpu
from jax.sharding import PartitionSpec as P

OB = 3
V = 512
NC = 4
QC = 512
HALF = 256
ROWS = OB * HALF
F32 = jnp.float32
BF16 = jnp.bfloat16
MESH = pl.DeviceIdType.MESH
GROUPS = (
    (0, 0, 128, 128),
    (0, 256, 128, 128),
    (1, 0, 384, 128),
    (2, 0, 256, 256),
    (3, 0, 128, 128),
    (3, 256, 128, 128),
)
PASSES = ((0, 0, 512), (1, 0, 512), (2, 0, 512), (3, 0, 256), (3, 256, 256))
SEQ = (
    ("j0", 0), ("j0", 1), ("j1a", 0), ("j1b", 0), ("j0", 2), ("j1c", 0), ("i1", 0), ("j1a", 1), ("j0", 4),
    ("j1c", 1), ("j1d", 0), ("i1", 1), ("j1d", 1), ("j1b", 1), ("j2a", 0), ("j1a", 2), ("j0", 3), ("j1c", 4),
    ("j1b", 2), ("j1d", 4), ("i2b", 0), ("j1d", 2), ("j1c", 2), ("j2b", 0), ("i1", 2), ("j2a", 1), ("j2b", 1),
    ("i2a", 0), ("j3a", 0), ("i2b", 1), ("j1b", 4), ("j1b", 3), ("i2a", 1), ("j3b", 0), ("j1c", 3),
    ("j1d", 3), ("j2a", 2), ("j1a", 3), ("j0", 5), ("i1", 3), ("j3a", 1), ("j2b", 2), ("j3c", 0), ("j3d", 0),
    ("j3b", 1), ("j3c", 1), ("j3d", 1), ("j1b", 5), ("j2a", 3), ("i1", 4), ("j1a", 4), ("j1a", 5), ("j2b", 3),
    ("i3", 0), ("i1", 5), ("i3", 1), ("j1c", 5), ("j4", 0), ("i2b", 3), ("j2b", 4), ("i2a", 3), ("j3c", 2),
    ("i4", 1), ("i2a", 2), ("j3a", 2), ("j1d", 5), ("j3d", 2), ("j4", 1), ("j2a", 4), ("i4", 0), ("i2b", 2),
    ("co0", 0), ("j3b", 2), ("co1", 0), ("j3b", 3), ("j2b", 5), ("i2b", 4), ("i2a", 4), ("i2a", 5),
    ("j2a", 5), ("j3c", 3), ("i3", 3), ("i2b", 5), ("j3a", 3), ("j3d", 3), ("i3", 2), ("i4", 3), ("j3b", 4),
    ("i3", 4), ("j3c", 4), ("j3d", 4), ("i4", 2), ("j4", 2), ("co0", 1), ("i3", 5), ("j3a", 4), ("co1", 1),
    ("j3a", 5), ("i4", 4), ("j3c", 5), ("i4", 5), ("j3d", 5), ("j4", 3), ("co0", 2), ("j3b", 5), ("co1", 2),
    ("j4", 4), ("co0", 3), ("co1", 3), ("j4", 5),
)
NG = len(GROUPS)


def kernel(
    raw_hbm, met_hbm, eocc_hbm, ev_hbm, out_hbm,
    raw_ref, eocc_ref, ev_ref, blocks, send, got, flat, evc, rden, fi, fj, met, acc, amp, gown, sib_s, sib_r, opp_s, opp_r, rs_s, rs_r, out_ref,
    met_sem, in_sem, all_s, all_r, ss, rs, gs, gr, out_sem,
):
    ia = lax.axis_index("ia")
    ja = lax.axis_index("ja")
    aux = lax.axis_index("aux")
    me = ia * 16 + ja * 2 + aux
    z, yh = ia >> 1, ia & 1
    x, core = ja >> 1, ja & 1
    y = yh * 2 + aux
    other = 1 - core

    def place(index):
        return {"ia": index >> 4, "ja": (index >> 1) & 7, "aux": index & 1}

    def step(v, d):
        return (v + (d + 4)) & 3

    def ydev(d):
        w = step(y, d)
        return {"ia": z * 2 + (w >> 1), "ja": ja, "aux": w & 1}

    def zdev(d):
        return {"ia": step(z, d) * 2 + yh, "ja": ja, "aux": aux}

    def xdev(d):
        return {"ia": ia, "ja": step(x, d) * 2 + core, "aux": aux}

    sib = {"ia": ia, "ja": x * 2 + other, "aux": aux}
    ypart = {"ia": ia, "ja": ja, "aux": 1 - aux}

    barrier = pltpu.get_barrier_semaphore()

    inputs = [
        pltpu.make_async_copy(raw_hbm, raw_ref, in_sem.at[0]),
        pltpu.make_async_copy(eocc_hbm, eocc_ref, in_sem.at[1]),
        pltpu.make_async_copy(ev_hbm, ev_ref, in_sem.at[2]),
    ]
    for copy in inputs:
        copy.start()

    def greet(i, carry):
        pl.semaphore_signal(barrier, inc=1, device_id=place(me ^ (127 - i)), device_id_type=MESH)
        return carry

    lax.fori_loop(0, 127, greet, 0)
    met_copies = [
        pltpu.make_async_copy(met_hbm.at[:, pl.ds(c * QC, QC)], met.at[c], met_sem.at[c])
        for c in range(NC)
    ]
    for c in range(NC):
        met_copies[c].start()

    for copy in inputs:
        copy.wait()
    pieces, occ = raw_ref.shape[0], raw_ref.shape[1]
    n = pieces * occ
    row = lax.broadcasted_iota(jnp.int32, (n, n), 0)
    col = lax.broadcasted_iota(jnp.int32, (n, n), 1)
    pick = ((row & 15) * occ + (row >> 4) == col).astype(F32).astype(BF16)
    by_occ = jnp.dot(pick, raw_ref[...].reshape(n, V), preferred_element_type=F32)
    lane = lax.broadcasted_iota(jnp.int32, (pieces, 128), 1)
    for t in range(8):
        for tile in range(4):
            rows = [
                by_occ[(OB * t + k) * 16 : (OB * t + k) * 16 + 16, tile * 128 : tile * 128 + 128]
                for k in range(OB)
            ]
            for q in range(4):
                a, b, c = [
                    r if k == q else pltpu.roll(r, (32 * (k - q)) % 128, 1)
                    for k, r in enumerate(rows)
                ]
                blocks[t * 16 + tile * 4 + q] = jnp.where(
                    lane < 32, a, jnp.where(lane < 64, b, jnp.where(lane < 96, c, 0.0))
                )
    for there in range(128):
        row_part = blocks[there]
        col_part = pltpu.roll(blocks[((there >> 1) & 7) * 16 + (there >> 4) * 2 + (there & 1)], 96, 1)
        upper = jnp.where(lane < 96, row_part, col_part)
        lower = jnp.where(lane[:8] < 64, col_part[:8], pltpu.roll(col_part[8:], 64, 1))
        send[there] = jnp.concatenate([upper, lower], axis=0).astype(BF16)

    pl.semaphore_wait(barrier, 127)
    mine = got.at[me]
    pltpu.make_async_copy(send.at[me], mine, all_r).start()

    def one(i, carry):
        there = me ^ (128 - i)
        pltpu.make_async_remote_copy(
            src_ref=send.at[there], dst_ref=mine, send_sem=all_s, recv_sem=all_r,
            device_id=place(there), device_id_type=MESH,
        ).start()
        return carry

    lax.fori_loop(1, 128, one, 0)

    for j in range(2):
        lanes = pl.ds(pl.multiple_of(aux * HALF + j * 128, 128), 128)
        evc[j * 128 : (j + 1) * 128] = jnp.broadcast_to(ev_ref[:, lanes], (128, 128)).T

    def invert(p, carry):
        k, l = lax.div(p, OB), lax.rem(p, OB)
        ei, ej = eocc_ref[OB * ia + k], eocc_ref[OB * ja + l]
        for tile in range(4):
            lanes = slice(tile * 128, tile * 128 + 128)
            rden[k, l, :, lanes] = 1.0 / (evc[...] + ev_ref[:, lanes] - ei - ej)
        return carry

    lax.fori_loop(0, OB * OB, invert, 0)

    def put(ref, g, i, dev):
        pltpu.make_async_remote_copy(
            src_ref=ref, dst_ref=ref, send_sem=ss.at[g, int(i > 12)], recv_sem=rs.at[g, i],
            device_id=dev, device_id_type=MESH,
        ).start()

    def arrived(ref, g, i):
        pltpu.make_async_copy(ref, ref, rs.at[g, i]).wait()

    every = slice(None)
    lo, hi = pl.ds(0, 16), pl.ds(16, 16)
    first2, last2 = pl.ds(0, 2), pl.ds(2, 2)
    yp, ym, y2 = step(y, 1), step(y, -1), step(y, 2)
    zp, zm, z2 = step(z, 1), step(z, -1), step(z, 2)
    xp, xm, x2 = step(x, 1), step(x, -1), step(x, 2)

    def fja(g, zz, yy, r=every):
        c, start, na, nb = GROUPS[g]
        return fj.at[c, :, zz, yy, r, pl.ds(start, na)]

    def fjb(g, zz, yy, r=every):
        c, start, na, nb = GROUPS[g]
        return fj.at[c, :, zz, yy, r, pl.ds(start + na, nb)]

    def fig(g, xx, cc, aa=every):
        c, start, na, nb = GROUPS[g]
        return fi.at[c, :, xx, cc, aa, :, pl.ds(start, na + nb)]

    def received():
        pltpu.make_async_copy(send, send, all_r).wait()
        for h in range(4):
            sources = slice(h * 32, h * 32 + 32)
            cells = got[sources].astype(F32)
            lower = cells[:, 16:24]
            rest = jnp.concatenate([lower, pltpu.roll(lower, 64, 2)], axis=1)
            lanes = slice(h * 512, h * 512 + 512)
            flat[0:128, lanes] = cells[:, 0:16].reshape(512, 128).astype(BF16).T
            flat[128:192, lanes] = rest.reshape(512, 128).astype(BF16).T[0:64]

    waited = set()

    def fit(g):
        c, start, na, nb = GROUPS[g]
        if c not in waited:
            met_copies[c].wait()
            waited.add(c)
        lanes = slice(start, start + na + nb)
        r = jnp.dot(flat[...], met[c, :, lanes], preferred_element_type=F32).astype(BF16)
        for k in range(OB):
            fi[c, k, x, core, aux, :, lanes] = r[32 * k : 32 * k + 32]
            fj[c, k, z, y, :, lanes] = r[96 + 32 * k : 128 + 32 * k]

    lone_src, lone_dst = (y + 1 + 2 * aux) & 3, (y + 3 + 2 * aux) & 3
    lone = {"ia": z * 2 + (lone_dst >> 1), "ja": ja, "aux": lone_dst & 1}
    middle2 = pl.ds(1, 2)

    def j0(g):
        fit(g)
        put(fja(g, z, y), g, 0, ydev(1))
        put(fja(g, z, y), g, 1, ydev(-1))
        put(fjb(g, z, y), g, 2, zdev(1))
        put(fjb(g, z, y), g, 3, zdev(-1))
        put(fig(g, x, core, aux), g, 13, ypart)

    def i1(g):
        arrived(fig(g, x, core, 1 - aux), g, 13)
        put(fig(g, x, core), g, 14, xdev(1))
        put(fig(g, x, core), g, 15, xdev(-1))
        put(fig(g, x, core), g, 17, sib)

    def j1a(g):
        arrived(fja(g, z, ym), g, 0)
        put(fja(g, z, ym, lo), g, 5, ydev(1))

    def j1b(g):
        arrived(fja(g, z, yp), g, 1)
        put(fja(g, z, yp, hi), g, 5, ydev(-1))

    def j1c(g):
        arrived(fjb(g, zm, y), g, 2)
        put(fjb(g, zm, y, lo), g, 6, zdev(1))

    def j1d(g):
        arrived(fjb(g, zp, y), g, 3)
        put(fjb(g, zp, y, hi), g, 6, zdev(-1))

    def j2a(g):
        arrived(fja(g, z, y2), g, 5)
        put(fja(g, z, every), g, 7, zdev(1))
        put(fja(g, z, every), g, 8, zdev(-1))

    def j2b(g):
        arrived(fjb(g, z2, y), g, 6)
        put(fjb(g, every, y), g, 9, ydev(1))
        put(fjb(g, every, y), g, 10, ydev(-1))

    def i2a(g):
        arrived(fig(g, xm, core), g, 14)
        put(fig(g, xm, core, 0), g, 16, xdev(1))
        put(fig(g, xm, core), g, 17, sib)

    def i2b(g):
        arrived(fig(g, xp, core), g, 15)
        put(fig(g, xp, core, 1), g, 16, xdev(-1))
        put(fig(g, xp, core), g, 17, sib)

    def j3a(g):
        arrived(fja(g, zm, every), g, 7)
        put(fja(g, zm, first2), g, 11, zdev(1))

    def j3b(g):
        arrived(fja(g, zp, every), g, 8)
        put(fja(g, zp, last2), g, 11, zdev(-1))

    def j3c(g):
        arrived(fjb(g, every, ym), g, 9)
        put(fjb(g, 0, ym), g, 12, ydev(1))

    def j3d(g):
        arrived(fjb(g, every, yp), g, 10)
        put(fjb(g, 3, yp), g, 12, ydev(-1))
        put(fjb(g, middle2, lone_src), g, 12, lone)

    def i3(g):
        arrived(fig(g, x2, core), g, 16)
        put(fig(g, x2, core), g, 17, sib)

    def i4(g):
        arrived(fig(g, every, other), g, 17)

    def j4(g):
        arrived(fja(g, z2, every), g, 11)
        arrived(fjb(g, every, y2), g, 12)

    over_q = (((1,), (1,)), ((), ()))

    half = pl.ds(2 * aux, 2)

    def direct(p):
        c, start, width = PASSES[p]
        lanes = slice(start, start + width)

        def one(l, carry):
            part = lax.dot_general(
                fi[c, :, half, :, :, :, lanes].reshape(ROWS, width),
                fj[c, l, :, :, :, lanes].reshape(V, width),
                over_q,
                preferred_element_type=F32,
            )
            for k in range(OB):
                value = 2.0 * part[k * HALF : (k + 1) * HALF]
                acc[k, l] = value if p == 0 else acc[k, l] + value
            return carry

        lax.fori_loop(0, OB, one, 0)

    def swapped(p, k):
        c, start, width = PASSES[p]
        lanes = slice(start, start + width)
        return lax.dot_general(
            fj[c, :, half, :, :, lanes].reshape(ROWS, width),
            fi[c, k, :, :, :, :, lanes].reshape(V, width),
            over_q,
            preferred_element_type=F32,
        )

    def swap(p):
        def one(k, carry):
            part = swapped(p, k)
            for l in range(OB):
                acc[k, l] = acc[k, l] - part[l * HALF : (l + 1) * HALF]
            return carry

        lax.fori_loop(0, OB, one, 0)

    steps = dict(
        j0=j0, i1=i1, j1a=j1a, j1b=j1b, j1c=j1c, j1d=j1d, j2a=j2a, j2b=j2b, i2a=i2a, i2b=i2b,
        j3a=j3a, j3b=j3b, j3c=j3c, j3d=j3d, i3=i3, i4=i4, j4=j4, co0=direct, co1=swap,
    )
    received()
    for name, g in SEQ:
        steps[name](g)

    def send_to(src, dst, kind, i, dev):
        pltpu.make_async_remote_copy(
            src_ref=src, dst_ref=dst, send_sem=gs.at[kind], recv_sem=gr.at[i],
            device_id=dev, device_id_type=MESH,
        ).start()

    def landed(dst, i):
        pltpu.make_async_copy(dst, dst, gr.at[i]).wait()

    plus, minus = pl.ds(0, 128), pl.ds(128, 128)
    rows_of = [pl.ds(k * HALF, HALF) for k in range(OB)]

    def amplitude(k):
        part = swapped(len(PASSES) - 1, k)
        for l in range(OB):
            value = (acc[k, l] - part[l * HALF : (l + 1) * HALF]) * rden[k, l]
            amp[k, :, l * V : (l + 1) * V] = value.astype(BF16)

    def gamma(m, block, ks, r, i):
        total = None
        for l in range(OB):
            value = jnp.dot(
                amp[ks, :, l * V : (l + 1) * V].reshape(-1, V),
                fj[block, l].reshape(V, QC),
                preferred_element_type=F32,
            )
            total = value if total is None else total + value
        low, high = total[:, :HALF], total[:, HALF:]
        sib_s[m, r] = jnp.where(core == 0, high, low).astype(BF16)
        send_to(sib_s.at[m, r], sib_r.at[m, r], 0, i, sib)
        gown[m, r] = jnp.where(core == 0, low, high)

    def near(m, k, block):
        gamma(m, block, slice(k, k + 1), rows_of[k], 3 * m + k)

    def far_send(k):
        r = rows_of[k]
        landed(sib_r.at[0, r], k)
        opp_s[r] = (gown[0, r] + sib_r[0, r].astype(F32)).astype(BF16)
        send_to(opp_s.at[r, plus], opp_r.at[r, plus], 1, 10 + k, xdev(1))
        send_to(opp_s.at[r, minus], opp_r.at[r, minus], 1, 13 + k, xdev(-1))

    def free(m, k):
        r, lanes, dev = rows_of[k], (minus, plus)[m - 1], xdev((1, -1)[m - 1])
        landed(sib_r.at[m, r], 3 * m + k)
        gown[m, r] = gown[m, r] + sib_r[m, r].astype(F32)
        rs_s[m - 1, r, lanes] = gown[m, r, lanes].astype(BF16)
        send_to(rs_s.at[m - 1, r, lanes], rs_r.at[m - 1, r, lanes], 2, 16 + k, dev)

    def relay(m, k):
        r, lanes, dev = rows_of[k], (plus, minus)[m - 1], xdev((1, -1)[m - 1])
        landed(opp_r.at[r, lanes], (10, 13)[m - 1] + k)
        rs_s[m - 1, r, lanes] = (gown[m, r, lanes] + opp_r[r, lanes].astype(F32)).astype(BF16)
        send_to(rs_s.at[m - 1, r, lanes], rs_r.at[m - 1, r, lanes], 2, 16 + k, dev)

    direct(len(PASSES) - 1)
    amplitude(0)
    near(0, 0, x2)
    near(1, 0, xp)
    far_send(0)
    near(2, 0, xm)
    free(1, 0)
    amplitude(1)
    near(0, 1, x2)
    free(2, 0)
    near(1, 1, xp)
    far_send(1)
    relay(1, 0)
    relay(2, 0)
    near(2, 1, xm)
    free(1, 1)
    amplitude(2)
    near(0, 2, x2)
    free(2, 1)
    near(1, 2, xp)
    far_send(2)
    relay(1, 1)
    relay(2, 1)
    near(2, 2, xm)
    free(1, 2)
    gamma(3, x, every, every, 9)
    free(2, 2)
    relay(1, 2)
    relay(2, 2)
    landed(sib_r.at[3], 9)
    gown[3] = gown[3] + sib_r[3].astype(F32)
    results = []
    for k in range(OB):
        r = rows_of[k]
        landed(rs_r.at[:, r], 16 + k)
        total = gown[3, r] + rs_r[0, r].astype(F32) + rs_r[1, r].astype(F32)
        for h in range(2):
            q = pl.ds(h * 128, 128)
            out_ref[k, q] = total[:, h * 128 : (h + 1) * 128].T
            results.append(pltpu.make_async_copy(out_ref.at[k, q], out_hbm.at[k, q], out_sem.at[k, h]))
            results[-1].start()
    def sent(rows, sem):
        size = met.at[0, pl.ds(0, rows)]
        pltpu.make_async_copy(size, size, sem).wait()

    for g in range(NG):
        for kind in range(2):
            sent(45 * (GROUPS[g][2] + GROUPS[g][3]) // 16, ss.at[g, kind])
    for kind, rows in enumerate((2 * ROWS, ROWS // 2, ROWS)):
        sent(rows, gs.at[kind])
    for copy in results:
        copy.wait()
    left = send.at[pl.ds(0, 127)]
    pltpu.make_async_copy(left, left, all_s).wait()


def body(raw_integrals, metric_root, eps_occ, eps_vir):
    pieces = raw_integrals.shape[0]
    aux_total = metric_root.shape[0]
    out = pl.pallas_call(
        kernel,
        out_shape=jax.ShapeDtypeStruct((OB, HALF, HALF), F32),
        in_specs=[pl.BlockSpec(memory_space=pltpu.HBM)] * 4,
        out_specs=pl.BlockSpec(memory_space=pltpu.HBM),
        scratch_shapes=[
            pltpu.VMEM(raw_integrals.shape, BF16),
            pltpu.SMEM(eps_occ.shape, F32),
            pltpu.VMEM((1, V), F32),
            pltpu.VMEM((128, pieces, 128), F32),
            pltpu.VMEM((128, 24, 128), BF16),
            pltpu.VMEM((128, 24, 128), BF16),
            pltpu.VMEM((192, aux_total), BF16),
            pltpu.VMEM((HALF, 128), F32),
            pltpu.VMEM((OB, OB, HALF, V), F32),
            pltpu.VMEM((NC, OB, 4, 2, 2, 32, QC), BF16),
            pltpu.VMEM((NC, OB, 4, 4, 32, QC), BF16),
            pltpu.VMEM((NC, aux_total, QC), BF16),
            pltpu.VMEM((OB, OB, HALF, V), F32),
            pltpu.VMEM((OB, HALF, OB * V), BF16),
            pltpu.VMEM((4, ROWS, HALF), F32),
            pltpu.VMEM((4, ROWS, HALF), BF16),
            pltpu.VMEM((4, ROWS, HALF), BF16),
            pltpu.VMEM((ROWS, HALF), BF16),
            pltpu.VMEM((ROWS, HALF), BF16),
            pltpu.VMEM((2, ROWS, HALF), BF16),
            pltpu.VMEM((2, ROWS, HALF), BF16),
            pltpu.VMEM((OB, HALF, HALF), F32),
            pltpu.SemaphoreType.DMA((NC,)),
            pltpu.SemaphoreType.DMA((3,)),
            pltpu.SemaphoreType.DMA,
            pltpu.SemaphoreType.DMA,
            pltpu.SemaphoreType.DMA((NG, 2)),
            pltpu.SemaphoreType.DMA((NG, 18)),
            pltpu.SemaphoreType.DMA((3,)),
            pltpu.SemaphoreType.DMA((19,)),
            pltpu.SemaphoreType.DMA((OB, 2)),
        ],
        compiler_params=pltpu.CompilerParams(
            collective_id=0, has_side_effects=True, vmem_limit_bytes=60 * 1024 * 1024
        ),
    )(raw_integrals, metric_root, eps_occ, eps_vir.reshape(1, V))
    return out.transpose(1, 0, 2)


def solution(mesh):
    in_specs = (P(("ia", "ja", "aux"), None, None), P(), P(), P())
    out_specs = P("ja", "ia", "aux")
    return jax.shard_map(body, mesh=mesh, in_specs=in_specs, out_specs=out_specs, check_vma=False)
```

time: 243 us -> 93.7 us (0.39)
  waiting for transfers between devices: 110 us -> 0 us
  Pallas kernels: 0 us -> 91.5 us
  blocking collectives: 72.7 us -> 0 us
  matrix products: 24.8 us -> 0 us
  local copies, waits for them, and re-layouts: 20.5 us -> 2.06 us
  between operations: 13.6 us -> 0.01 us
    all_gather x2 -> x0, waiting for transfers between devices: 110 us -> none  [the longest x1 55.6 us: body(): block_j = lax.all_gather(col_block, ('ia', 'aux'), axis=2, tiled=True)]
    pallas_call x0 -> x1, Pallas kernels: none -> 91.5 us  [body(): pl.pallas_call(kernel, out_shape=jax.ShapeDtypeStruct((OB, HALF, HALF), F...]
    all_to_all x2 -> x0, blocking collectives: 72.7 us -> none  [the longest x1 41.8 us: summed_on_arrival(): lax.all_to_all(pieces, axis, split_axis=0, concat_axis=0, tiled=True)]
    dot_general x4 -> x0, matrix products: 24.8 us -> none  [the longest x1 8.44 us: body(): lax.dot_general(flat_i, half_j.reshape(aux_total, OB * half_width), contr...]
    reshape x7 -> x0, local copies, waits for them, and re-layouts: 16 us -> none  [the longest x2 7.46 us: body(): raw_integrals.reshape(pieces, ia_count, OB, ia_count, aux_count, narrow)]
  transfers between devices with their start and end apart: 2 -> 0, of which waited for: 2 -> 0; matrix products, arithmetic and copies ran while one was open for 0% -> 0% of each run, Pallas kernels for 0% -> 0%
where the time goes in v3:
time: 93.7 us; the launch traced here: 93.6 us
  Pallas kernels  91.5 us (98%)
  local copies, waits for them, and re-layouts  2.06 us (2%)
    pallas_call x1, Pallas kernels, body(): pl.pallas_call(kernel, out_shape=jax.ShapeDtypeStruct((OB, HALF, HALF), F...  91.5 us
    unnamed x1, local copies, waits for them, and re-layouts  2.06 us

profile of v3, /device:TPU:1, one launch (start us, length us, event | category | flops | bytes accessed | tf_op | source)
XLA Modules:
  0.0 93.6 jit_solution(884948919882521692)
XLA Ops:
  0.0 91.5 %shard_map.46 = f32[3,256,256]{2,1,0:T(8,128)} custom-call(bf16[16,24,512]{2,1,0:T(8,128)(2,1)} %raw_hbm.1, bf16[2048,2048]{1,0:T(8,128)(2,1)} %met_hbm.1, f32[24]{0:T(128)} %eocc_hbm.1, f32[1,512]{1,0:T(1,128)} %bitcast.3), custom_call_target="tpu_custom_call" | custom-call | tf_op jit(solution)/shard_map/pallas_call | solution.py:454
  91.5 2.1 %copy.6 = f32[256,3,256]{2,0,1:T(8,128)} copy(f32[256,3,256]{2,0,1:T(8,128)} %bitcast.2) | data formatting | bytes 1572864

commit v4 on v3

--- a/solution.py
+++ b/solution.py
@@ -22,21 +22,21 @@
     (3, 0, 128, 128),
     (3, 256, 128, 128),
 )
-PASSES = ((0, 0, 512), (1, 0, 512), (2, 0, 512), (3, 0, 256), (3, 256, 256))
+PASSES = ((0, 0, 256), (0, 256, 256), (1, 0, 512), (2, 0, 512), (3, 0, 256), (3, 256, 256))
 SEQ = (
-    ("j0", 0), ("j0", 1), ("j1a", 0), ("j1b", 0), ("j0", 2), ("j1c", 0), ("i1", 0), ("j1a", 1), ("j0", 4),
-    ("j1c", 1), ("j1d", 0), ("i1", 1), ("j1d", 1), ("j1b", 1), ("j2a", 0), ("j1a", 2), ("j0", 3), ("j1c", 4),
-    ("j1b", 2), ("j1d", 4), ("i2b", 0), ("j1d", 2), ("j1c", 2), ("j2b", 0), ("i1", 2), ("j2a", 1), ("j2b", 1),
-    ("i2a", 0), ("j3a", 0), ("i2b", 1), ("j1b", 4), ("j1b", 3), ("i2a", 1), ("j3b", 0), ("j1c", 3),
-    ("j1d", 3), ("j2a", 2), ("j1a", 3), ("j0", 5), ("i1", 3), ("j3a", 1), ("j2b", 2), ("j3c", 0), ("j3d", 0),
-    ("j3b", 1), ("j3c", 1), ("j3d", 1), ("j1b", 5), ("j2a", 3), ("i1", 4), ("j1a", 4), ("j1a", 5), ("j2b", 3),
-    ("i3", 0), ("i1", 5), ("i3", 1), ("j1c", 5), ("j4", 0), ("i2b", 3), ("j2b", 4), ("i2a", 3), ("j3c", 2),
-    ("i4", 1), ("i2a", 2), ("j3a", 2), ("j1d", 5), ("j3d", 2), ("j4", 1), ("j2a", 4), ("i4", 0), ("i2b", 2),
-    ("co0", 0), ("j3b", 2), ("co1", 0), ("j3b", 3), ("j2b", 5), ("i2b", 4), ("i2a", 4), ("i2a", 5),
-    ("j2a", 5), ("j3c", 3), ("i3", 3), ("i2b", 5), ("j3a", 3), ("j3d", 3), ("i3", 2), ("i4", 3), ("j3b", 4),
-    ("i3", 4), ("j3c", 4), ("j3d", 4), ("i4", 2), ("j4", 2), ("co0", 1), ("i3", 5), ("j3a", 4), ("co1", 1),
-    ("j3a", 5), ("i4", 4), ("j3c", 5), ("i4", 5), ("j3d", 5), ("j4", 3), ("co0", 2), ("j3b", 5), ("co1", 2),
-    ("j4", 4), ("co0", 3), ("co1", 3), ("j4", 5),
+    ("j0", 0), ("j0", 1), ("j1a", 0), ("j1b", 0), ("j0", 2), ("j1c", 0), ("j1b", 1), ("i1", 0), ("j1d", 0),
+    ("j1c", 1), ("j1d", 1), ("j1a", 1), ("j0", 4), ("j2a", 0), ("j1a", 2), ("j1b", 2), ("j1c", 2), ("j1d", 2),
+    ("j0", 3), ("j2b", 0), ("i1", 1), ("j0", 5), ("j1c", 4), ("j1d", 4), ("j2a", 1), ("i1", 2), ("j1c", 3),
+    ("j3b", 0), ("i2b", 0), ("j1b", 3), ("j1d", 5), ("j1b", 4), ("j1d", 3), ("j2a", 2), ("j1a", 3),
+    ("j2b", 2), ("i2a", 0), ("j2b", 1), ("j1b", 5), ("i1", 4), ("j3a", 0), ("j3c", 0), ("i1", 3), ("j3d", 0),
+    ("j1a", 4), ("j2b", 3), ("j2a", 3), ("j3c", 2), ("i2b", 4), ("j1a", 5), ("j3d", 2), ("i2b", 2),
+    ("j3b", 2), ("i2a", 2), ("j1c", 5), ("j3a", 2), ("j4", 0), ("i3", 0), ("j3b", 1), ("j3c", 1), ("i2a", 1),
+    ("i2b", 1), ("j3d", 1), ("i2a", 4), ("i2a", 3), ("j3a", 1), ("i2b", 3), ("i4", 0), ("j2b", 4), ("co0", 0),
+    ("j2a", 4), ("co1", 0), ("j2b", 5), ("j3b", 3), ("i3", 1), ("j3c", 3), ("j4", 2), ("i3", 2), ("i1", 5),
+    ("j3a", 3), ("j3d", 3), ("j2a", 5), ("i3", 4), ("j4", 1), ("i4", 1), ("co0", 1), ("i3", 3), ("co1", 1),
+    ("j3c", 4), ("i4", 2), ("co0", 2), ("j3b", 4), ("j3a", 4), ("j3d", 4), ("co1", 2), ("j3c", 5), ("i4", 3),
+    ("j3d", 5), ("i2a", 5), ("i2b", 5), ("j4", 3), ("co0", 3), ("j3b", 5), ("j3a", 5), ("co1", 3), ("i4", 4),
+    ("j4", 4), ("i3", 5), ("co0", 4), ("co1", 4), ("i4", 5), ("j4", 5),
 )
 NG = len(GROUPS)
 
@@ -84,11 +84,8 @@
     for copy in inputs:
         copy.start()
 
-    def greet(i, carry):
-        pl.semaphore_signal(barrier, inc=1, device_id=place(me ^ (127 - i)), device_id_type=MESH)
-        return carry
-
-    lax.fori_loop(0, 127, greet, 0)
+    for o in range(127, 0, -1):
+        pl.semaphore_signal(barrier, inc=1, device_id=me ^ o, device_id_type=pl.DeviceIdType.LOGICAL)
     met_copies = [
         pltpu.make_async_copy(met_hbm.at[:, pl.ds(c * QC, QC)], met.at[c], met_sem.at[c])
         for c in range(NC)
@@ -131,10 +128,10 @@
     pltpu.make_async_copy(send.at[me], mine, all_r).start()
 
     def one(i, carry):
-        there = me ^ (128 - i)
+        there = me ^ ((i * 37) & 127)
         pltpu.make_async_remote_copy(
             src_ref=send.at[there], dst_ref=mine, send_sem=all_s, recv_sem=all_r,
-            device_id=place(there), device_id_type=MESH,
+            device_id=there, device_id_type=pl.DeviceIdType.LOGICAL,
         ).start()
         return carry
 
@@ -296,7 +293,7 @@
         c, start, width = PASSES[p]
         lanes = slice(start, start + width)
 
-        def one(l, carry):
+        for l in range(OB):
             part = lax.dot_general(
                 fi[c, :, half, :, :, :, lanes].reshape(ROWS, width),
                 fj[c, l, :, :, :, lanes].reshape(V, width),
@@ -306,9 +303,6 @@
             for k in range(OB):
                 value = 2.0 * part[k * HALF : (k + 1) * HALF]
                 acc[k, l] = value if p == 0 else acc[k, l] + value
-            return carry
-
-        lax.fori_loop(0, OB, one, 0)
 
     def swapped(p, k):
         c, start, width = PASSES[p]
@@ -321,13 +315,10 @@
         )
 
     def swap(p):
-        def one(k, carry):
+        for k in range(OB):
             part = swapped(p, k)
             for l in range(OB):
                 acc[k, l] = acc[k, l] - part[l * HALF : (l + 1) * HALF]
-            return carry
-
-        lax.fori_loop(0, OB, one, 0)
 
     steps = dict(
         j0=j0, i1=i1, j1a=j1a, j1b=j1b, j1c=j1c, j1d=j1d, j2a=j2a, j2b=j2b, i2a=i2a, i2b=i2b,

time: 93.7 us -> 89.5 us (0.955)
  Pallas kernels: 91.5 us -> 87.2 us
    pallas_call x1, Pallas kernels: 91.5 us -> 87.2 us  [body(): pl.pallas_call(kernel, out_shape=jax.ShapeDtypeStruct((OB, HALF, HALF), F...]
where the time goes in v4:
time: 89.5 us; the launch traced here: 89.3 us
  Pallas kernels  87.2 us (97%)
  local copies, waits for them, and re-layouts  2.06 us (2%)
    pallas_call x1, Pallas kernels, body(): pl.pallas_call(kernel, out_shape=jax.ShapeDtypeStruct((OB, HALF, HALF), F...  87.2 us
    unnamed x1, local copies, waits for them, and re-layouts  2.06 us

profile of v4, /device:TPU:1, one launch (start us, length us, event | category | flops | bytes accessed | tf_op | source)
XLA Modules:
  0.0 89.3 jit_solution(5573784086457829278)
XLA Ops:
  0.0 87.2 %shard_map.46 = f32[3,256,256]{2,1,0:T(8,128)} custom-call(bf16[16,24,512]{2,1,0:T(8,128)(2,1)} %raw_hbm.1, bf16[2048,2048]{1,0:T(8,128)(2,1)} %met_hbm.1, f32[24]{0:T(128)} %eocc_hbm.1, f32[1,512]{1,0:T(1,128)} %bitcast.3), custom_call_target="tpu_custom_call" | custom-call | tf_op jit(solution)/shard_map/pallas_call | solution.py:445
  87.2 2.1 %copy.6 = f32[256,3,256]{2,0,1:T(8,128)} copy(f32[256,3,256]{2,0,1:T(8,128)} %bitcast.2) | data formatting | bytes 1572864

commit v5 on v4

--- a/solution.py
+++ b/solution.py
@@ -128,7 +128,7 @@
     pltpu.make_async_copy(send.at[me], mine, all_r).start()
 
     def one(i, carry):
-        there = me ^ ((i * 37) & 127)
+        there = me ^ ((i * 53) & 127)
         pltpu.make_async_remote_copy(
             src_ref=send.at[there], dst_ref=mine, send_sem=all_s, recv_sem=all_r,
             device_id=there, device_id_type=pl.DeviceIdType.LOGICAL,

time: 89.5 us -> 88.6 us (0.990)
  no operation moved by 1% of the time
where the time goes in v5:
time: 88.6 us; the launch traced here: 88.4 us
  Pallas kernels  86.4 us (98%)
  local copies, waits for them, and re-layouts  2.06 us (2%)
    pallas_call x1, Pallas kernels, body(): pl.pallas_call(kernel, out_shape=jax.ShapeDtypeStruct((OB, HALF, HALF), F...  86.4 us
    unnamed x1, local copies, waits for them, and re-layouts  2.06 us

profile of v5, /device:TPU:1, one launch (start us, length us, event | category | flops | bytes accessed | tf_op | source)
XLA Modules:
  0.0 88.4 jit_solution(6448229378558514043)
XLA Ops:
  0.0 86.4 %shard_map.46 = f32[3,256,256]{2,1,0:T(8,128)} custom-call(bf16[16,24,512]{2,1,0:T(8,128)(2,1)} %raw_hbm.1, bf16[2048,2048]{1,0:T(8,128)(2,1)} %met_hbm.1, f32[24]{0:T(128)} %eocc_hbm.1, f32[1,512]{1,0:T(1,128)} %bitcast.3), custom_call_target="tpu_custom_call" | custom-call | tf_op jit(solution)/shard_map/pallas_call | solution.py:445
  86.4 2.1 %copy.6 = f32[256,3,256]{2,0,1:T(8,128)} copy(f32[256,3,256]{2,0,1:T(8,128)} %bitcast.2) | data formatting | bytes 1572864
